TPU v7x, 32 devices: a whole 2x2x4 slice. The times are simulated.
32 devices in a mesh: query: 4 (over y, x), cand: 2 (over core), tensor: 4 (over z).
Axes of the slice: x: 2, y: 2, z: 4, core: 2. Of those that a mesh axis runs over, the one named last changes fastest.
Arguments:
- cand_states: bfloat16 [8192, 2048], P(('query', 'cand'), 'tensor'), parts along dimension 0, may hold values from -6 to 6
- prefix_states: bfloat16 [256, 2048], P(('query', 'cand'), 'tensor'), parts along dimension 0, may hold values from -6 to 6
- norm_gain: float32 [2048], replicated, may hold values from 0.5 to 1.5
- w_query: bfloat16 [2048, 1024], P(None, 'tensor'), may hold values from -1 to 1
- w_key: bfloat16 [2048, 256], P(None, 'tensor'), may hold values from -1 to 1
- w_value: bfloat16 [2048, 256], P(None, 'tensor'), may hold values from -0.125 to 0.125
- w_out: bfloat16 [1024, 2048], P('tensor'), may hold values from -1.5 to 1.5
- cand_lengths: int32 [64], P(('query', 'cand')), parts along dimension 0, may hold values from 32 to 128, as said below
Outputs:
- attn_out: bfloat16 [8192, 2048], P(('query', 'cand', 'tensor')), parts along dimension 0
There are 4 independent parts, one for each index of `query`. A program takes and returns all parts, laid end to end along the dimension named above; an argument that names none is the same for every part. Nothing has to cross between parts.
Inputs may be any that keep to these rules, and one draw needn't show every extreme that they name: `cand_lengths`: some candidate has all 128 slots live.
All inputs are finite; a program needn't handle non-finite values.
Results may differ from a plain program's by a relative error of at most 0.013.
Values may be sent and summed in bfloat16 or wider, within the bound.
No kernel may reach another device: no remote copies, remote signals or barrier semaphores. Data moves between devices by JAX's collectives and lax.ppermute only.
A program may use at most 64 MiB of HBM per device.

v0:
```python
import jax
import jax.numpy as jnp
from jax import lax
from jax.sharding import PartitionSpec as P

epsilon = 1e-06
theta_base = 10000.0


def rotate(values, positions):
    half_size = values.shape[-1] // 2
    frequency = theta_base ** (-jnp.arange(half_size, dtype=jnp.float32) * 2.0 / values.shape[-1])
    angles = positions.astype(jnp.float32)[:, None] * frequency[None, :]
    cosine = jnp.cos(angles)
    sine_part = jnp.sin(angles)
    lower_half = values[:, :half_size]
    upper_half = values[:, half_size:]
    return jnp.concatenate(
        [
            lower_half * cosine - upper_half * sine_part,
            upper_half * cosine + lower_half * sine_part,
        ],
        axis=-1,
    )


def normalize(states, norm_gain):
    values = states.astype(jnp.float32)
    square = jnp.mean(values * values, axis=-1, keepdims=True)
    return (values * lax.rsqrt(square + epsilon) * norm_gain[None, :]).astype(jnp.bfloat16)


def self_scores_of(queries, cand_keys):
    scores = jnp.einsum("cqd,ckd->cqk", queries, cand_keys, preferred_element_type=jnp.float32)
    slots = jnp.arange(scores.shape[1], dtype=jnp.int32)
    causal = slots[:, None] >= slots[None, :]
    return jnp.where(causal[None], scores, -jnp.inf)


def body(cand_states, prefix_states, norm_gain, w_query, w_key, w_value, w_out, cand_lengths):
    cand_full, prefix_full = (
        lax.all_gather(cand_states, "tensor", axis=1, tiled=True),
        lax.all_gather(prefix_states, "tensor", axis=1, tiled=True),
    )
    normed_cand = normalize(cand_full, norm_gain)
    normed_prefix = normalize(prefix_full, norm_gain)
    cand_count = cand_lengths.shape[0]
    cand_len = cand_full.shape[0] // cand_count
    prefix_rows = prefix_full.shape[0]
    cand_groups = lax.axis_size("cand")
    tensor_size = lax.axis_size("tensor")
    prefix_len = prefix_rows * cand_groups
    head_size = w_query.shape[1]
    cand_pos = prefix_len + jnp.tile(jnp.arange(cand_len, dtype=jnp.int32), cand_count)
    cand_key = jnp.dot(normed_cand, w_key, preferred_element_type=jnp.float32).astype(jnp.bfloat16)
    cand_value = jnp.dot(normed_cand, w_value, preferred_element_type=jnp.float32).astype(
        jnp.bfloat16
    )
    prefix_key = jnp.dot(normed_prefix, w_key, preferred_element_type=jnp.float32).astype(
        jnp.bfloat16
    )
    prefix_value = jnp.dot(normed_prefix, w_value, preferred_element_type=jnp.float32).astype(
        jnp.bfloat16
    )
    query_rows = rotate(
        jnp.dot(normed_cand, w_query, preferred_element_type=jnp.float32), cand_pos
    ) * head_size ** (-0.5)
    queries = query_rows.astype(jnp.bfloat16).reshape(cand_count, cand_len, head_size)
    cand_key, cand_value = (
        lax.all_gather(cand_key, "tensor", axis=1, tiled=True),
        lax.all_gather(cand_value, "tensor", axis=1, tiled=True),
    )
    key_pieces, value_pieces = (
        lax.all_gather(prefix_key, ("cand", "tensor"), axis=0, tiled=True),
        lax.all_gather(prefix_value, ("cand", "tensor"), axis=0, tiled=True),
    )

    def arrange(pieces):
        blocks = pieces.reshape(cand_groups, tensor_size, prefix_rows, pieces.shape[1])
        return blocks.transpose(0, 2, 1, 3).reshape(prefix_len, pieces.shape[1] * tensor_size)

    prefix_pos = jnp.arange(prefix_len, dtype=jnp.int32)
    prefix_keys = rotate(arrange(key_pieces).astype(jnp.float32), prefix_pos).astype(jnp.bfloat16)
    prefix_values = arrange(value_pieces)
    cand_keys = (
        rotate(cand_key.astype(jnp.float32), cand_pos)
        .astype(jnp.bfloat16)
        .reshape(cand_count, cand_len, head_size)
    )
    cand_values = cand_value.reshape(cand_count, cand_len, head_size)
    self_scores = self_scores_of(queries, cand_keys)
    prefix_scores = jnp.einsum(
        "cqd,kd->cqk", queries, prefix_keys, preferred_element_type=jnp.float32
    )
    highest = jnp.maximum(self_scores.max(-1), prefix_scores.max(-1))
    self_weights = jnp.exp(self_scores - highest[..., None])
    prefix_weights = jnp.exp(prefix_scores - highest[..., None])
    divisor = self_weights.sum(-1) + prefix_weights.sum(-1)
    summed = jnp.einsum(
        "cqk,ckd->cqd",
        self_weights.astype(jnp.bfloat16),
        cand_values,
        preferred_element_type=jnp.float32,
    )
    summed = summed + jnp.einsum(
        "cqk,kd->cqd",
        prefix_weights.astype(jnp.bfloat16),
        prefix_values,
        preferred_element_type=jnp.float32,
    )
    slots = jnp.arange(cand_len, dtype=jnp.int32)
    live_rows = slots[None, :] < cand_lengths[:, None]
    head_rows = jnp.where(live_rows[..., None], summed / divisor[..., None], 0.0)
    head_rows = head_rows.reshape(cand_count * cand_len, head_size).astype(jnp.bfloat16)
    row_count = head_rows.shape[0] // tensor_size
    all_heads = lax.all_to_all(head_rows, "tensor", split_axis=0, concat_axis=1, tiled=True)
    full_out = lax.all_gather(w_out, "tensor", axis=0, tiled=True)
    summed_out = jnp.zeros((row_count, full_out.shape[1]), jnp.float32)
    for head_index in range(tensor_size):
        head_term = jnp.dot(
            all_heads[:, head_index * head_size : (head_index + 1) * head_size],
            full_out[head_index * head_size : (head_index + 1) * head_size],
            preferred_element_type=jnp.float32,
        )
        summed_out = summed_out + lax.optimization_barrier(head_term.astype(jnp.bfloat16)).astype(
            jnp.float32
        )
    return summed_out.astype(jnp.bfloat16)


def solution(mesh):
    in_specs = (
        P(("query", "cand"), "tensor"),
        P(("query", "cand"), "tensor"),
        P(),
        P(None, "tensor"),
        P(None, "tensor"),
        P(None, "tensor"),
        P("tensor", None),
        P(("query", "cand")),
    )
    out_specs = P(("query", "cand", "tensor"), None)
    return jax.shard_map(body, mesh=mesh, in_specs=in_specs, out_specs=out_specs, check_vma=False)
```

profile of v0, /device:TPU:0, one launch (start us, length us, event | category | flops | bytes accessed | tf_op | source)
XLA Modules:
  0.0 214.7 jit_solution(11699257511544938787)
XLA Ops:
  6.5 0.0 copy-start
  6.5 0.0 copy-start.6
  6.5 0.0 copy-start.7
  6.5 0.0 all-gather.3.cloned.1.call-start
  6.5 0.7 all-gather.3.cloned.1.call-update
  7.3 0.0 all-gather.5.cloned.1.call-start
  7.3 0.7 all-gather.5.cloned.1.call-update
  8.0 15.3 %all_gather.23 = bf16[32,2048]{1,0:T(8,128)(2,1)S(1)} all-gather(bf16[32,512]{1,0:T(8,128)(2,1)} %param.9), channel_id=1, replica_groups=mesh['query'=4,'cand'=2,'tensor'=4] {'tensor'}, dimensions={1}, use_global_device_ids=true | all-gather | bytes 163840 | tf_op jit(solution)/shard_map/all_gather | solution.py:43
  23.3 0.1 fusion.30
  23.5 1.2 convolution_convert_fusion.7
  24.7 26.7 %all_gather.24 = bf16[256,64]{1,0:T(8,128)(2,1)S(1)} all-gather(bf16[32,64]{1,0:T(8,128)(2,1)S(1)} %convolution_convert_fusion.7), channel_id=1, replica_groups=mesh['query'=4,'cand'=2,'tensor'=4] {'cand','tensor'}, dimensions={0}, use_global_device_ids=true | all-gather | bytes 36864 | tf_op jit(solution)/shard_map/all_gather | solution.py:74
  51.4 0.1 copy.21
  51.5 0.1 reshape.111
  51.6 1.2 convolution_convert_fusion.6
  52.8 27.9 %all_gather.26 = bf16[256,64]{1,0:T(8,128)(2,1)S(1)} all-gather(bf16[32,64]{1,0:T(8,128)(2,1)S(1)} %convolution_convert_fusion.6), channel_id=1, replica_groups=mesh['query'=4,'cand'=2,'tensor'=4] {'cand','tensor'}, dimensions={0}, use_global_device_ids=true | all-gather | bytes 36864 | tf_op jit(solution)/shard_map/all_gather | solution.py:75
  80.8 0.1 reshape.114
  81.0 0.0 copy-done.7
  81.0 0.1 iota_compare_fusion.1
  81.1 0.2 fusion.51
  81.3 13.3 %all-gather.3.cloned.1.call-done = bf16[1024,2048]{1,0:T(8,128)(2,1)} async-done(((bf16[1024,512]{1,0:T(8,128)(2,1)}), bf16[1024,2048]{1,0:T(8,128)(2,1)}) %all-gather.3.cloned.1.call-update) | async-done | bytes 4194320 | tf_op jit(solution)/shard_map/all_gather | solution.py:42
  94.6 0.0 copy-start.2
  94.6 3.2 %fusion = f32[1024]{0:T(1024)S(1)} fusion(bf16[1024,2048]{1,0:T(8,128)(2,1)} %all-gather.3.cloned.1.call-done), kind=kLoop, calls=%fused_computation.2 | loop fusion | flops 6290432 | bytes 4198400 | tf_op jit(solution)/shard_map/reduce_sum | solution.py:29
  97.8 0.0 copy-done.6
  97.8 0.2 copy-done.2
  98.0 0.0 copy-start.4
  98.0 1.0 fusion.2
  99.0 0.0 copy-start.1
  99.1 2.0 copy-done.1
  101.0 0.0 copy-done.4
  101.0 0.0 copy-start.5
  101.0 1.4 convolution_convert_fusion.5
  102.4 21.4 %all_gather.22 = bf16[1024,256]{0,1:T(8,128)(2,1)S(1)} all-gather(bf16[1024,64]{0,1:T(8,128)(2,1)S(1)} %convolution_convert_fusion.5), channel_id=1, replica_groups=mesh['query'=4,'cand'=2,'tensor'=4] {'tensor'}, dimensions={1}, use_global_device_ids=true | all-gather | bytes 655360 | tf_op jit(solution)/shard_map/all_gather | solution.py:70
  123.8 0.2 copy.20
  124.0 0.1 convert_element_type.144
  124.1 0.0 copy-done.5
  124.1 3.6 %convolution_convert_fusion.4 = bf16[1024,64]{0,1:T(8,128)(2,1)S(1)} fusion(bf16[1024,2048]{1,0:T(8,128)(2,1)} %copy-done.1, bf16[2048,64]{0,1:T(8,128)(2,1)S(1)} %copy-done.5), kind=kOutput, calls=%fused_computation.15 | convolution fusion | flops 268500992 | bytes 4587520 | tf_op jit(solution)/shard_map/dot_general | solution.py:56
  127.7 21.3 %all_gather.25 = bf16[1024,256]{0,1:T(8,128)(2,1)S(1)} all-gather(bf16[1024,64]{0,1:T(8,128)(2,1)S(1)} %convolution_convert_fusion.4), channel_id=1, replica_groups=mesh['query'=4,'cand'=2,'tensor'=4] {'tensor'}, dimensions={1}, use_global_device_ids=true | all-gather | bytes 655360 | tf_op jit(solution)/shard_map/all_gather | solution.py:71
  149.0 0.2 copy.27
  149.2 0.0 copy-done
  149.2 3.5 %fusion.67 = f32[1024,256]{1,0:T(8,128)S(1)} fusion(bf16[1024,2048]{1,0:T(8,128)(2,1)} %copy-done.1, bf16[2048,256]{1,0:T(8,128)(2,1)S(1)} %copy-done), kind=kOutput, calls=%fused_computation.92 | convolution fusion | flops 1073741824 | bytes 6291456 | tf_op jit(solution)/shard_map/dot_general | solution.py:66
  152.7 2.5 %fusion.19 = (f32[1024,128]{1,0:T(8,128)S(1)}, f32[1024,128]{1,0:T(8,128)S(1)}, bf16[1024,128]{1,0:T(8,128)(2,1)S(1)}, bf16[1024,128]{1,0:T(8,128)(2,1)S(1)}) fusion(f32[1024,256]{1,0:T(8,128)S(1)} %fusion.67, f32[128]{0:T(128)S(1)} %multiply_power_fusion, f32[1024]{0:T(1024)S(1)} %convert_bitcast_fusion.1, f32[1024,256]{1,0:T(8,128)S(1)} %convert_element_type.144), kind=kLoop, calls=%fused_computation.35 | loop fusion | flops 1966080 | bytes 3674624 | tf_op jit(solution)/shard_map/sub | solution.py:20
  155.2 0.3 fusion.66
  155.5 0.3 fusion.65
  155.8 0.1 fusion.36
  155.9 0.1 fusion.28
  156.0 0.3 fusion.33
  156.3 0.4 fusion.5
  156.8 1.0 copy.25
  157.8 5.3 %all-to-all-start = ((bf16[4,256,256]{1,2,0:T(8,128)(2,1)}), bf16[4,256,256]{1,2,0:T(8,128)(2,1)S(1)}, u32[]{:S(2)}, u32[]{:S(2)}) async-start(bf16[4,256,256]{1,2,0:T(8,128)(2,1)} %copy.25), calls=%async_computation | async-start | bytes 1048576 | tf_op jit(solution)/shard_map/all_to_all | solution.py:116
  163.1 38.6 %all-gather.5.cloned.1.call-done = bf16[1024,2048]{1,0:T(8,128)(2,1)} async-done(((bf16[256,2048]{1,0:T(8,128)(2,1)}), bf16[1024,2048]{1,0:T(8,128)(2,1)}) %all-gather.5.cloned.1.call-update) | async-done | bytes 4194320 | tf_op jit(solution)/shard_map/all_gather | solution.py:117
  201.7 0.0 all-to-all-done
  201.7 0.0 copy-start.3
  201.7 1.8 convolution_convert_fusion.3
  203.6 1.7 convolution_convert_fusion.2
  205.3 0.0 copy-done.3
  205.3 0.5 convolution_convert_fusion.1
  205.7 0.5 convolution_convert_fusion
  206.2 1.7 add_convert_fusion
  (10 shorter events, 0.1 us)
Async XLA Ops:
  6.5 142.7 %copy-start = (bf16[2048,256]{1,0:T(8,128)(2,1)S(1)}, bf16[2048,256]{1,0:T(8,128)(2,1)}, u32[]{:S(2)}) copy-start(bf16[2048,256]{1,0:T(8,128)(2,1)} %param.11) | copy-start | bytes 3145732
  6.5 91.3 %copy-start.6 = (f32[2048]{0:T(1024)S(1)}, f32[2048]{0:T(1024)}, u32[]{:S(2)}) copy-start(f32[2048]{0:T(1024)} %param.10) | copy-start | bytes 24580
  6.5 74.5 %copy-start.7 = (s32[8]{0:T(128)S(1)}, s32[8]{0:T(128)}, u32[]{:S(2)}) copy-start(s32[8]{0:T(128)} %param.15) | copy-start | bytes 100
  6.5 88.0 %all-gather.3.cloned.1.call-start = ((), (), s32[]{:S(2)}) async-start(), calls=%async_computation.1 | async-start | bytes 5242880 | tf_op jit(solution)/shard_map/all_gather | solution.py:42
  7.3 194.5 %all-gather.5.cloned.1.call-start = ((), (), s32[]{:S(2)}) async-start(), calls=%async_computation.2 | async-start | bytes 5242880 | tf_op jit(solution)/shard_map/all_gather | solution.py:117
  94.6 3.4 %copy-start.2 = (bf16[1024,2048]{1,0:T(8,128)(2,1)S(1)}, bf16[1024,2048]{1,0:T(8,128)(2,1)}, u32[]{:S(2)}) copy-start(bf16[1024,2048]{1,0:T(8,128)(2,1)} %all-gather.3.cloned.1.call-done) | copy-start | bytes 12582916
  98.0 3.0 %copy-start.4 = (bf16[2048,64]{0,1:T(8,128)(2,1)S(1)}, bf16[2048,64]{0,1:T(8,128)(2,1)}, u32[]{:S(2)}) copy-start(bf16[2048,64]{0,1:T(8,128)(2,1)} %param.12) | copy-start | bytes 786436
  99.0 2.0 copy-start.1
  101.0 23.0 %copy-start.5 = (bf16[2048,64]{0,1:T(8,128)(2,1)S(1)}, bf16[2048,64]{0,1:T(8,128)(2,1)}, u32[]{:S(2)}) copy-start(bf16[2048,64]{0,1:T(8,128)(2,1)} %param.13) | copy-start | bytes 786436
  157.8 44.0 %all-to-all-start = ((bf16[4,256,256]{1,2,0:T(8,128)(2,1)}), bf16[4,256,256]{1,2,0:T(8,128)(2,1)S(1)}, u32[]{:S(2)}, u32[]{:S(2)}) async-start(bf16[4,256,256]{1,2,0:T(8,128)(2,1)} %copy.25), calls=%async_computation | async-start | bytes 1048576 | tf_op jit(solution)/shard_map/all_to_all | solution.py:116
  201.7 3.5 %copy-start.3 = (bf16[1024,2048]{1,0:T(8,128)(2,1)S(1)}, bf16[1024,2048]{1,0:T(8,128)(2,1)}, u32[]{:S(2)}) copy-start(bf16[1024,2048]{1,0:T(8,128)(2,1)} %all-gather.5.cloned.1.call-done) | copy-start | bytes 12582916
Sparse Core Ops, SparseCore 0:
  8.9 85.6 all-gather.2
  96.1 105.5 all-gather.4
where the time goes:
time: 215 us
  blocking collectives  113 us (53%)
  waiting for transfers between devices  53.3 us (25%)
  matrix products  16.8 us (8%)
  between operations  13.6 us (6%)
  other arithmetic  9.09 us (4%)
  starting transfers between devices  5.36 us (2%)
  local copies, waits for them, and re-layouts  3.97 us (2%)
    all_gather x1, waiting for transfers between devices, body(): full_out = lax.all_gather(w_out, 'tensor', axis=0, tiled=True)  38.6 us
    all_gather x1, blocking collectives, body(): lax.all_gather(prefix_value, ('cand', 'tensor'), axis=0, tiled=True)  27.9 us
    all_gather x1, blocking collectives, body(): lax.all_gather(prefix_key, ('cand', 'tensor'), axis=0, tiled=True)  26.7 us
    all_gather x1, blocking collectives, body(): lax.all_gather(cand_key, 'tensor', axis=1, tiled=True)  21.4 us
    all_gather x1, blocking collectives, body(): lax.all_gather(cand_value, 'tensor', axis=1, tiled=True)  21.3 us
    all_gather x1, blocking collectives, body(): lax.all_gather(prefix_states, 'tensor', axis=1, tiled=True)  15.3 us
    all_gather x1, waiting for transfers between devices, body(): lax.all_gather(cand_states, 'tensor', axis=1, tiled=True)  13.3 us
    all_to_all x1, starting transfers between devices, body(): lax.all_to_all(head_rows, 'tensor', split_axis=0, concat_axis=1, tiled=True)  5.32 us
  transfers between devices with their start and end apart: 3, of which 2 were waited for; matrix products, arithmetic and copies ran while one was open for 10% of the time, Pallas kernels for 0%

commit v1 on v0

--- a/solution.py
+++ b/solution.py
@@ -114,7 +114,13 @@
     head_rows = head_rows.reshape(cand_count * cand_len, head_size).astype(jnp.bfloat16)
     row_count = head_rows.shape[0] // tensor_size
     all_heads = lax.all_to_all(head_rows, "tensor", split_axis=0, concat_axis=1, tiled=True)
-    full_out = lax.all_gather(w_out, "tensor", axis=0, tiled=True)
+    count = lax.axis_size("tensor")
+    moving, tiles = (w_out, [w_out])
+    for _ in range(count - 1):
+        moving = lax.ppermute(moving, "tensor", [(i, (i + 1) % count) for i in range(count)])
+        tiles.insert(0, moving)
+    line = jnp.concatenate(tiles, axis=0)
+    full_out = jnp.roll(line, (lax.axis_index("tensor") + 1) * w_out.shape[0], axis=0)
     summed_out = jnp.zeros((row_count, full_out.shape[1]), jnp.float32)
     for head_index in range(tensor_size):
         head_term = jnp.dot(

time: 215 us -> 305 us (1.42)
  blocking collectives: 113 us -> 169 us
  starting transfers between devices: 5.36 us -> 23.8 us
  local copies, waits for them, and re-layouts: 3.97 us -> 20.9 us
  waiting for transfers between devices: 53.3 us -> 42 us
  other arithmetic: 9.09 us -> 15.4 us
    all_gather x1, blocking collectives: 15.3 us -> 69.7 us  [body(): lax.all_gather(prefix_states, 'tensor', axis=1, tiled=True)]
    all_gather x1 -> x0, waiting for transfers between devices: 38.6 us -> none  [body(): full_out = lax.all_gather(w_out, 'tensor', axis=0, tiled=True)]
    ppermute x0 -> x3, waiting for transfers between devices: none -> 37.6 us  [body(): lax.ppermute(moving, 'tensor', [(i, (i + 1) % count) for i in range(count)])]
    ppermute x0 -> x3, starting transfers between devices: none -> 19.5 us  [body(): lax.ppermute(moving, 'tensor', [(i, (i + 1) % count) for i in range(count)])]
    all_gather x1, blocking collectives: 27.9 us -> 42.9 us  [body(): lax.all_gather(prefix_value, ('cand', 'tensor'), axis=0, tiled=True)]
    all_gather x1, waiting for transfers between devices: 13.3 us -> 0.01 us  [body(): lax.all_gather(cand_states, 'tensor', axis=1, tiled=True)]
    unnamed x16 -> x25, local copies, waits for them, and re-layouts: 2.19 us -> 13.2 us
    all_gather x1, blocking collectives: 21.4 us -> 15.7 us  [body(): lax.all_gather(cand_key, 'tensor', axis=1, tiled=True)]
  transfers between devices with their start and end apart: 3 -> 5, of which waited for: 2 -> 2; matrix products, arithmetic and copies ran while one was open for 10% -> 6% of each run, Pallas kernels for 0% -> 0%
where the time goes in v1:
time: 305 us; the launch traced here: 304 us
  blocking collectives  169 us (55%)
  waiting for transfers between devices  42 us (14%)
  starting transfers between devices  23.8 us (8%)
  local copies, waits for them, and re-layouts  20.9 us (7%)
  matrix products  18.9 us (6%)
  other arithmetic  15.4 us (5%)
  between operations  13.6 us (4%)
    all_gather x1, blocking collectives, body(): lax.all_gather(prefix_states, 'tensor', axis=1, tiled=True)  69.7 us
    all_gather x1, blocking collectives, body(): lax.all_gather(prefix_value, ('cand', 'tensor'), axis=0, tiled=True)  42.9 us
    ppermute x3, waiting for transfers between devices, body(): lax.ppermute(moving, 'tensor', [(i, (i + 1) % count) for i in range(count)])  37.6 us
    all_gather x1, blocking collectives, body(): lax.all_gather(prefix_key, ('cand', 'tensor'), axis=0, tiled=True)  23.8 us
    ppermute x3, starting transfers between devices, body(): lax.ppermute(moving, 'tensor', [(i, (i + 1) % count) for i in range(count)])  19.5 us
    all_gather x1, blocking collectives, body(): lax.all_gather(cand_value, 'tensor', axis=1, tiled=True)  17 us
    all_gather x1, blocking collectives, body(): lax.all_gather(cand_key, 'tensor', axis=1, tiled=True)  15.7 us
    unnamed x25, local copies, waits for them, and re-layouts  13.2 us
  transfers between devices with their start and end apart: 5, of which 2 were waited for; matrix products, arithmetic and copies ran while one was open for 6% of the time, Pallas kernels for 0%

profile of v1, /device:TPU:0, one launch (start us, length us, event | category | flops | bytes accessed | tf_op | source)
XLA Modules:
  0.0 303.9 jit_solution(13000517315887828273)
XLA Ops:
  6.5 0.0 copy-start
  6.5 0.0 all-gather.2.cloned.1.call-start
  6.5 0.7 all-gather.2.cloned.1.call-update
  7.3 3.1 %collective-permute-start = (bf16[256,2048]{1,0:T(8,128)(2,1)}, bf16[256,2048]{1,0:T(8,128)(2,1)S(1)}, u32[]{:S(2)}, u32[]{:S(2)}) collective-permute-start(bf16[256,2048]{1,0:T(8,128)(2,1)} %param.14), channel_id=1, source_target_pairs={{0,1},{1,2},{2,3},{3,0},{4,5},{5,6},{6,7},{7,4},{8,9},{9,10},{10,1... | collective-permute-start | bytes 3145736 | tf_op jit(solution)/shard_map/ppermute | solution.py:120
  10.4 37.6 %collective-permute-done = bf16[256,2048]{1,0:T(8,128)(2,1)S(1)} collective-permute-done((bf16[256,2048]{1,0:T(8,128)(2,1)}, bf16[256,2048]{1,0:T(8,128)(2,1)S(1)}, u32[]{:S(2)}, u32[]{:S(2)}) %collective-permute-start) | collective-permute-done | bytes 1048608 | tf_op jit(solution)/shard_map/ppermute | solution.py:120
  47.9 14.7 %collective-permute-start.1 = (bf16[256,2048]{1,0:T(8,128)(2,1)S(1)}, bf16[256,2048]{1,0:T(8,128)(2,1)}, u32[]{:S(2)}, u32[]{:S(2)}) collective-permute-start(bf16[256,2048]{1,0:T(8,128)(2,1)S(1)} %collective-permute-done), channel_id=1, source_target_pairs={{0,1},{1,2},{2,3},{3,0},{4,5},{5,6},{6,7},{7,4},{8,9},{9,10},{10,1... | collective-permute-start | bytes 3145736 | tf_op jit(solution)/shard_map/ppermute | solution.py:120
  62.7 69.7 %all_gather.20 = bf16[32,2048]{1,0:T(8,128)(2,1)S(1)} all-gather(bf16[32,512]{1,0:T(8,128)(2,1)} %param.9), channel_id=1, replica_groups=mesh['query'=4,'cand'=2,'tensor'=4] {'tensor'}, dimensions={1}, use_global_device_ids=true | all-gather | bytes 163840 | tf_op jit(solution)/shard_map/all_gather | solution.py:43
  132.4 0.1 fusion.30
  132.6 1.2 convolution_convert_fusion.7
  133.8 23.8 %all_gather.21 = bf16[256,64]{1,0:T(8,128)(2,1)S(1)} all-gather(bf16[32,64]{1,0:T(8,128)(2,1)S(1)} %convolution_convert_fusion.7), channel_id=1, replica_groups=mesh['query'=4,'cand'=2,'tensor'=4] {'cand','tensor'}, dimensions={0}, use_global_device_ids=true | all-gather | bytes 36864 | tf_op jit(solution)/shard_map/all_gather | solution.py:74
  157.7 0.1 copy.21
  157.7 0.1 reshape.111
  157.9 0.0 collective-permute-done.1
  157.9 1.6 collective-permute-start.2
  159.5 1.2 convolution_convert_fusion.6
  160.7 42.9 %all_gather.23 = bf16[256,64]{1,0:T(8,128)(2,1)S(1)} all-gather(bf16[32,64]{1,0:T(8,128)(2,1)S(1)} %convolution_convert_fusion.6), channel_id=1, replica_groups=mesh['query'=4,'cand'=2,'tensor'=4] {'cand','tensor'}, dimensions={0}, use_global_device_ids=true | all-gather | bytes 36864 | tf_op jit(solution)/shard_map/all_gather | solution.py:75
  203.7 0.1 reshape.114
  203.8 0.6 iota_compare_fusion
  204.4 1.3 iota_compare_fusion.1
  205.7 0.2 fusion.51
  206.0 0.0 collective-permute-done.2
  206.0 2.3 constant_dynamic-update-slice_fusion.7
  208.3 2.3 constant_dynamic-update-slice_fusion.6
  210.6 1.1 constant_dynamic-update-slice_fusion.5
  211.7 0.0 copy-done.2
  211.7 1.1 constant_dynamic-update-slice_fusion.4
  212.8 3.1 %fusion = f32[1024]{0:T(1024)S(1)} fusion(bf16[1024,2048]{1,0:T(8,128)(2,1)} %all-gather.2.cloned.1.call-done), kind=kLoop, calls=%fused_computation.2 | loop fusion | flops 6290432 | bytes 4198400 | tf_op jit(solution)/shard_map/reduce_sum | solution.py:29
  216.0 0.0 copy-done.7
  216.0 3.2 %fusion.2 = bf16[1024,2048]{1,0:T(8,128)(2,1)S(1)} fusion(bf16[1024,2048]{1,0:T(8,128)(2,1)} %all-gather.2.cloned.1.call-done, f32[2048]{0:T(1024)S(1)} %copy-done.7, f32[1024]{0:T(1024)S(1)} %add_rsqrt_fusion), kind=kLoop, calls=%fused_computation.4 | loop fusion | flops 8388608 | bytes 8400896 | tf_op jit(solution)/shard_map/convert_element_type | solution.py:30
  219.2 0.0 copy-done.4
  219.2 0.0 copy-start.1
  219.2 1.4 convolution_convert_fusion.4
  220.6 0.5 copy-done.1
  221.1 0.0 copy-done.5
  221.2 1.4 convolution_convert_fusion.5
  222.5 17.0 %all_gather.22 = bf16[1024,256]{0,1:T(8,128)(2,1)} all-gather(bf16[1024,64]{0,1:T(8,128)(2,1)S(1)} %convolution_convert_fusion.4), channel_id=1, replica_groups=mesh['query'=4,'cand'=2,'tensor'=4] {'tensor'}, dimensions={1}, use_global_device_ids=true | all-gather | bytes 655360 | tf_op jit(solution)/shard_map/all_gather | solution.py:71
  239.6 2.1 copy.27
  241.7 0.0 copy-done
  241.7 4.4 %fusion.71 = f32[1024,256]{1,0:T(8,128)} fusion(bf16[1024,2048]{1,0:T(8,128)(2,1)} %copy-done.1, bf16[2048,256]{1,0:T(8,128)(2,1)S(1)} %copy-done), kind=kOutput, calls=%fused_computation.104 | convolution fusion | flops 1073741824 | bytes 6291456 | tf_op jit(solution)/shard_map/dot_general | solution.py:66
  246.1 15.7 %all_gather.19 = bf16[1024,256]{0,1:T(8,128)(2,1)} all-gather(bf16[1024,64]{0,1:T(8,128)(2,1)S(1)} %convolution_convert_fusion.5), channel_id=1, replica_groups=mesh['query'=4,'cand'=2,'tensor'=4] {'tensor'}, dimensions={1}, use_global_device_ids=true | all-gather | bytes 655360 | tf_op jit(solution)/shard_map/all_gather | solution.py:70
  261.8 2.1 copy.20
  263.9 1.2 convert_element_type.144
  265.1 3.8 %fusion.19 = (f32[1024,128]{1,0:T(8,128)S(1)}, f32[1024,128]{1,0:T(8,128)S(1)}, bf16[1024,128]{1,0:T(8,128)(2,1)S(1)}, bf16[1024,128]{1,0:T(8,128)(2,1)S(1)}) fusion(f32[1024,256]{1,0:T(8,128)} %fusion.71, f32[128]{0:T(128)S(1)} %multiply_power_fusion, f32[1024]{0:T(1024)S(1)} %convert_bitcast_fusion.1, f32[1024,256]{1,0:T(8,128)S(1)} %convert_element_type.144), kind=kLoop, calls=%fused_computation.35 | loop fusion | flops 1966080 | bytes 3674624 | tf_op jit(solution)/shard_map/sub | solution.py:20
  268.9 0.3 fusion.70
  269.2 0.0 copy-done.6
  269.2 0.3 fusion.69
  269.6 0.1 fusion.28
  269.6 0.0 copy-done.3
  269.7 0.4 fusion.33
  270.0 0.1 fusion.36
  270.1 0.0 copy-done.8
  270.1 1.2 fusion.5
  271.3 2.1 copy.25
  273.4 4.3 %all-to-all-start = ((bf16[4,256,256]{1,2,0:T(8,128)(2,1)}), bf16[4,256,256]{1,2,0:T(8,128)(2,1)}, u32[]{:S(2)}, u32[]{:S(2)}) async-start(bf16[4,256,256]{1,2,0:T(8,128)(2,1)} %copy.25), calls=%async_computation | async-start | bytes 1048576 | tf_op jit(solution)/shard_map/all_to_all | solution.py:116
  277.8 2.3 constant_dynamic-update-slice_fusion.3
  280.1 2.3 constant_dynamic-update-slice_fusion.2
  282.4 1.1 constant_dynamic-update-slice_fusion.1
  283.5 1.1 constant_dynamic-update-slice_fusion
  284.6 3.7 %all-to-all-done = bf16[4,256,256]{1,2,0:T(8,128)(2,1)} async-done(((bf16[4,256,256]{1,2,0:T(8,128)(2,1)}), bf16[4,256,256]{1,2,0:T(8,128)(2,1)}, u32[]{:S(2)}, u32[]{:S(2)}) %all-to-all-start) | async-done | bytes 524320 | tf_op jit(solution)/shard_map/all_to_all | solution.py:116
  288.3 1.8 convolution_convert_fusion.3
  290.1 1.8 convolution_convert_fusion
  291.8 1.8 convolution_convert_fusion.1
  293.6 1.8 convolution_convert_fusion.2
  295.4 1.7 add_convert_fusion
  (17 shorter events, 0.1 us)
Async XLA Ops:
  6.5 235.1 %copy-start = (bf16[2048,256]{1,0:T(8,128)(2,1)S(1)}, bf16[2048,256]{1,0:T(8,128)(2,1)}, u32[]{:S(2)}) copy-start(bf16[2048,256]{1,0:T(8,128)(2,1)} %param.11) | copy-start | bytes 3145732
  6.5 205.2 %copy-start.2 = (bf16[256,2048]{1,0:T(8,128)(2,1)S(1)}, bf16[256,2048]{1,0:T(8,128)(2,1)}, u32[]{:S(2)}) copy-start(bf16[256,2048]{1,0:T(8,128)(2,1)} %param.14) | copy-start | bytes 3145732
  6.5 209.4 %copy-start.7 = (f32[2048]{0:T(1024)S(1)}, f32[2048]{0:T(1024)}, u32[]{:S(2)}) copy-start(f32[2048]{0:T(1024)} %param.10) | copy-start | bytes 24580
  6.5 206.3 %all-gather.2.cloned.1.call-start = ((), (), s32[]{:S(2)}) async-start(), calls=%async_computation.1 | async-start | bytes 5242880 | tf_op jit(solution)/shard_map/all_gather | solution.py:42
  7.3 40.7 %collective-permute-start = (bf16[256,2048]{1,0:T(8,128)(2,1)}, bf16[256,2048]{1,0:T(8,128)(2,1)S(1)}, u32[]{:S(2)}, u32[]{:S(2)}) collective-permute-start(bf16[256,2048]{1,0:T(8,128)(2,1)} %param.14), channel_id=1, source_target_pairs={{0,1},{1,2},{2,3},{3,0},{4,5},{5,6},{6,7},{7,4},{8,9},{9,10},{10,1... | collective-permute-start | bytes 3145736 | tf_op jit(solution)/shard_map/ppermute | solution.py:120
  47.9 109.9 %collective-permute-start.1 = (bf16[256,2048]{1,0:T(8,128)(2,1)S(1)}, bf16[256,2048]{1,0:T(8,128)(2,1)}, u32[]{:S(2)}, u32[]{:S(2)}) collective-permute-start(bf16[256,2048]{1,0:T(8,128)(2,1)S(1)} %collective-permute-done), channel_id=1, source_target_pairs={{0,1},{1,2},{2,3},{3,0},{4,5},{5,6},{6,7},{7,4},{8,9},{9,10},{10,1... | collective-permute-start | bytes 3145736 | tf_op jit(solution)/shard_map/ppermute | solution.py:120
  157.9 48.1 %collective-permute-start.2 = (bf16[256,2048]{1,0:T(8,128)(2,1)}, bf16[256,2048]{1,0:T(8,128)(2,1)}, u32[]{:S(2)}, u32[]{:S(2)}) collective-permute-start(bf16[256,2048]{1,0:T(8,128)(2,1)} %collective-permute-done.1), channel_id=1, source_target_pairs={{0,1},{1,2},{2,3},{3,0},{4,5},{5,6},{6,7},{7,4},{8,9},{9,10},{10,1... | collective-permute-start | bytes 3145736 | tf_op jit(solution)/shard_map/ppermute | solution.py:120
  210.6 8.6 %copy-start.4 = (bf16[2048,64]{0,1:T(8,128)(2,1)S(1)}, bf16[2048,64]{0,1:T(8,128)(2,1)}, u32[]{:S(2)}) copy-start(bf16[2048,64]{0,1:T(8,128)(2,1)} %param.13) | copy-start | bytes 786436
  212.8 8.3 %copy-start.5 = (bf16[2048,64]{0,1:T(8,128)(2,1)S(1)}, bf16[2048,64]{0,1:T(8,128)(2,1)}, u32[]{:S(2)}) copy-start(bf16[2048,64]{0,1:T(8,128)(2,1)} %param.12) | copy-start | bytes 786436
  219.2 1.9 copy-start.1
  239.6 29.6 %copy-start.6 = (pred[128,128]{0,1:T(8,128)(4,1)S(1)}, pred[128,128]{0,1:T(8,128)(4,1)}, u32[]{:S(2)}) copy-start(pred[128,128]{0,1:T(8,128)(4,1)} %iota_compare_fusion) | copy-start | bytes 49156
  246.1 24.0 %copy-start.8 = (pred[8,128]{1,0:T(8,128)(4,1)S(1)}, pred[8,128]{1,0:T(8,128)(4,1)}, u32[]{:S(2)}) copy-start(pred[8,128]{1,0:T(8,128)(4,1)} %iota_compare_fusion.1) | copy-start | bytes 3076
  263.9 5.8 %copy-start.3 = (bf16[1024,256]{1,0:T(8,128)(2,1)S(1)}, bf16[1024,256]{1,0:T(8,128)(2,1)}, u32[]{:S(2)}) copy-start(bf16[1024,256]{1,0:T(8,128)(2,1)} %copy.27) | copy-start | bytes 1572868
  273.4 14.9 %all-to-all-start = ((bf16[4,256,256]{1,2,0:T(8,128)(2,1)}), bf16[4,256,256]{1,2,0:T(8,128)(2,1)}, u32[]{:S(2)}, u32[]{:S(2)}) async-start(bf16[4,256,256]{1,2,0:T(8,128)(2,1)} %copy.25), calls=%async_computation | async-start | bytes 1048576 | tf_op jit(solution)/shard_map/all_to_all | solution.py:116
Sparse Core Ops, SparseCore 0:
  8.9 118.1 all-gather.1
